TPU v7x, 32 devices: a whole 2x2x4 slice. The times are simulated.
32 devices in a mesh: runner: 4 (over z), cells: 8 (over y, x, core).
Axes of the slice: x: 2, y: 2, z: 4, core: 2. Of those that a mesh axis runs over, the one named last changes fastest.
Arguments:
- states: float32 [512, 64, 128], P('runner', 'cells'), may hold values from -4 to 4
- diffusivity: float32 [64, 128], P('cells'), may hold values from 0.03 to 0.2
- velocity: float32 [2, 64, 128], P(None, 'cells'), may hold values from -0.15 to 0.15
- counts: int32 [4], replicated, may hold values from 1 to 128, 256 in all
- obs_index: int32 [4096], P('cells'), may hold values from 0 to 1023
- obs_value: float32 [4096], P('cells'), may hold values from -6 to 6
- obs_weight: float32 [4096], P('cells'), may hold values from 0.3 to 3
Outputs:
- analysed: float32 [512, 64, 128], P('runner', 'cells')
Inputs may be any that keep to these rules, and one draw needn't show every extreme that they name: Runner r's members fill its first counts[r] slots, in runner order; the counts sum to 256 and the largest is exactly 128. Observation k lies in the rows of cells index k // 512; obs_index counts cells within those 8 x 128 cells, row by row; a cell may be observed more than once.
All inputs are finite; a program needn't handle non-finite values.
Results may differ from a plain program's by a relative error of at most 0.013.
Values may be sent and summed in bfloat16 or wider, within the bound.
No kernel may reach another device: no remote copies, remote signals or barrier semaphores. Data moves between devices by JAX's collectives and lax.ppermute only.
A program may use at most 64 MiB of HBM per device.

v0:
```python
import jax
import jax.numpy as jnp
from jax import lax
from jax.sharding import PartitionSpec as P

STEPS = 4


def with_halo(block, sides, width):
    for axis, dim in sides:
        count = lax.axis_size(axis)
        forward = [(i, i + 1) for i in range(count - 1)]
        forward.append((count - 1, 0))
        backward = [(target, source) for source, target in forward]
        low = lax.ppermute(
            lax.slice_in_dim(block, block.shape[dim] - width, None, axis=dim), axis, forward
        )
        high = lax.ppermute(lax.slice_in_dim(block, 0, width, axis=dim), axis, backward)
        block = jnp.concatenate([low, block, high], axis=dim)
    return block


def update(values, upper_row, lower_row, diffusivity, velocity_rows, velocity_cols):
    right_col = jnp.roll(values, -1, axis=2)
    left_col = jnp.roll(values, 1, axis=2)
    laplace = upper_row + lower_row + right_col + left_col - 4.0 * values
    return (
        values
        + diffusivity * laplace
        - 0.5 * velocity_rows * (upper_row - lower_row)
        - 0.5 * velocity_cols * (right_col - left_col)
        - 0.05 * values * values * values
    )


def body(states, diffusivity, velocity, counts, obs_index, obs_value, obs_weight):
    runners = lax.axis_size("runner")
    slot_count = states.shape[0]
    rows_own = states.shape[1]
    members = slot_count // 2 * runners
    values = states
    extended = with_halo(values, (("cells", 1),), STEPS)
    fields = jnp.concatenate([diffusivity[None], velocity], axis=0)
    wide_fields = with_halo(fields, (("cells", 1),), STEPS)
    for iteration in range(STEPS):
        inner = extended.shape[1] - 2
        first = iteration + 1
        local = wide_fields[:, first : first + inner, :]
        extended = update(
            extended[:, 1:-1, :],
            extended[:, 2:, :],
            extended[:, :-2, :],
            local[0],
            local[1],
            local[2],
        )
    values = extended
    runner_rank = lax.axis_index("runner")
    run_ends = jnp.cumsum(counts)
    offsets = run_ends - counts
    run_ids = jnp.arange(runners, dtype=jnp.int32)
    picker = run_ids == runner_rank
    own_count = jnp.sum(jnp.where(picker, counts, 0))
    own_base = jnp.sum(jnp.where(picker, offsets, 0))
    position = jnp.arange(slot_count, dtype=jnp.int32)
    is_live = position < own_count
    flat_rows = values.reshape(slot_count, -1)
    live_sum = jnp.sum(jnp.where(is_live[:, None], flat_rows, 0.0), axis=0)
    ensemble_mean = lax.psum(live_sum, "runner") / members
    member_deviation = jnp.where(is_live[:, None], flat_rows - ensemble_mean, 0.0).astype(
        jnp.bfloat16
    )
    member_ids = jnp.arange(members, dtype=jnp.int32)
    owner_run = jnp.sum((run_ends[None, :] <= member_ids[:, None]).astype(jnp.int32), axis=1)
    owner_off = jnp.sum(
        jnp.where(owner_run[:, None] == run_ids[None, :], offsets[None, :], 0), axis=1
    )
    slot_of = owner_run * slot_count + member_ids - owner_off
    own_obs = jnp.take(member_deviation, obs_index, axis=1)
    gathered = lax.all_gather(member_deviation, "runner", axis=0, tiled=True)
    compact = jnp.take(gathered, slot_of, axis=0)
    observed = jnp.take(compact, obs_index, axis=1)
    weighted = (own_obs.astype(jnp.float32) * obs_weight).astype(jnp.bfloat16)
    gram_part = lax.dot_general(
        weighted, observed, (((1,), (1,)), ((), ())), preferred_element_type=jnp.float32
    )
    innovation = obs_value - jnp.take(ensemble_mean, obs_index)
    bias_part = jnp.dot(weighted.astype(jnp.float32), innovation, precision=lax.Precision.HIGHEST)
    gram_rows, bias_rows = lax.psum((gram_part, bias_part), "cells")
    member_col = own_base + position
    trace_sum = lax.psum(
        jnp.sum(weighted.astype(jnp.float32) * own_obs.astype(jnp.float32)), ("runner", "cells")
    )
    scaling = members / trace_sum
    scaled_own = (gram_rows * scaling).astype(jnp.bfloat16)
    bias_own = (bias_rows * scaling).astype(jnp.bfloat16)
    scaled_all, bias_all = (
        lax.all_gather(scaled_own, "runner", axis=0, tiled=True),
        lax.all_gather(bias_own, "runner", axis=0, tiled=True),
    )
    scaled_full = jnp.take(scaled_all, slot_of, axis=0)
    bias_full = jnp.take(bias_all, slot_of, axis=0)
    square = jnp.dot(scaled_own, scaled_full, preferred_element_type=jnp.float32).astype(
        jnp.bfloat16
    )
    cubed = jnp.dot(square, scaled_full, preferred_element_type=jnp.float32)
    identity = jnp.where(
        is_live[:, None] & (member_ids[None, :] == member_col[:, None]), 1.0, 0.0
    ).astype(jnp.float32)
    transform = (
        1.0 * identity
        - 0.5 * scaled_own.astype(jnp.float32)
        + 0.375 * square.astype(jnp.float32)
        - 0.3125 * cubed
    )
    shift_weights = jnp.dot(
        transform, bias_full.astype(jnp.float32), precision=lax.Precision.HIGHEST
    )
    increment = lax.psum(
        jnp.dot(
            shift_weights, member_deviation.astype(jnp.float32), precision=lax.Precision.HIGHEST
        ),
        "runner",
    )
    narrow = transform.astype(jnp.bfloat16)
    applied = jnp.dot(narrow, compact, preferred_element_type=jnp.float32)
    result = jnp.where(is_live[:, None], ensemble_mean + increment + applied, 0.0)
    return result.reshape(slot_count, rows_own, -1)


def solution(mesh):
    return jax.shard_map(
        body,
        mesh=mesh,
        in_specs=(
            P("runner", "cells", None),
            P("cells", None),
            P(None, "cells", None),
            P(),
            P("cells"),
            P("cells"),
            P("cells"),
        ),
        out_specs=P("runner", "cells", None),
        check_vma=False,
    )
```

profile of v0, /device:TPU:0, one launch (start us, length us, event | category | flops | bytes accessed | tf_op | source)
XLA Modules:
  0.0 205.1 jit_solution(15974762030387377627)
XLA Ops:
  7.8 2.9 %collective-permute-start.3 = (f32[3,4,128]{2,1,0:T(4,128)S(1)}, f32[3,4,128]{2,1,0:T(4,128)S(1)}, u32[]{:S(2)}, u32[]{:S(2)}) collective-permute-start(f32[3,4,128]{2,1,0:T(4,128)S(1)} %get-tuple-element.41), channel_id=1, source_target_pairs={{1,0},{2,1},{3,2},{4,3},{5,4},{6,5},{7,6},{0,7},{9,8},{10,9},{11,1... | collective-permute-start | bytes 18440 | tf_op jit(solution)/shard_map/ppermute | solution.py:18
  10.7 1.3 fusion.41
  12.1 2.6 %collective-permute-start.1 = (f32[128,4,128]{2,1,0:T(4,128)S(1)}, f32[128,4,128]{2,1,0:T(4,128)S(1)}, u32[]{:S(2)}, u32[]{:S(2)}) collective-permute-start(f32[128,4,128]{2,1,0:T(4,128)S(1)} %get-tuple-element.30), channel_id=1, source_target_pairs={{1,0},{2,1},{3,2},{4,3},{5,4},{6,5},{7,6},{0,7},{9,8},{10,9},{11,1... | collective-permute-start | bytes 786440 | tf_op jit(solution)/shard_map/ppermute | solution.py:18
  17.9 2.1 %collective-permute-done = f32[128,4,128]{2,1,0:T(4,128)S(1)} collective-permute-done((f32[128,4,128]{2,1,0:T(4,128)S(1)}, f32[128,4,128]{2,1,0:T(4,128)S(1)}, u32[]{:S(2)}, u32[]{:S(2)}) %collective-permute-start) | collective-permute-done | bytes 262176 | tf_op jit(solution)/shard_map/ppermute | solution.py:15
  20.9 1.2 fusion.3
  22.8 1.2 fusion.4
  24.7 1.2 fusion.5
  27.0 13.4 %psum.35 = f32[1024]{0:T(1024)S(1)} all-reduce(f32[1024]{0:T(1024)S(1)} %bitcast.75), channel_id=1, replica_groups=mesh['runner'=4,'cells'=8] {'runner'}, use_global_device_ids=true, to_apply=%region_2.3 | all-reduce | flops 1024 | bytes 8192 | tf_op jit(solution)/shard_map/psum | solution.py:69
  41.3 0.8 copy-done
  42.3 2.3 %gather_fusion.4 = f32[512]{0:T(512)S(1)} fusion(f32[1024]{0:T(1024)S(1)} %broadcast_multiply_fusion, s32[1024]{0:T(1024)S(1)} %pad_clamp_fusion.1), kind=kCustom, calls=%fused_computation.4 | custom fusion | bytes 6144 | tf_op jit(solution)/shard_map/jit(_take)/gather | solution.py:87
  44.6 1.3 gather_fusion
  46.8 38.3 %psum.37 = f32[]{:T(128)} all-reduce(f32[]{:T(128)} %fusion.10), channel_id=1, replica_groups=mesh['runner'=4,'cells'=8] {'runner','cells'}, use_global_device_ids=true, to_apply=%region_9.10 | all-reduce | flops 1 | bytes 8 | tf_op jit(solution)/shard_map/psum | solution.py:91
  86.1 12.9 %psum.38 = f32[128]{0:T(128)S(1)} all-reduce(f32[128]{0:T(128)S(1)} %convolution_bitcast_fusion), channel_id=1, replica_groups=mesh['runner'=4,'cells'=8] {'cells'}, use_global_device_ids=true, to_apply=%region_10.11 | all-reduce | flops 128 | bytes 1024 | tf_op jit(solution)/shard_map/psum | solution.py:89
  99.0 9.9 %all-gather = bf16[4,1,128]{2,1,0:T(2,128)(2,1)S(1)} all-gather(bf16[1,1,128]{2,1,0:T(2,128)(2,1)S(1)} %convert_bitcast_fusion), channel_id=1, replica_groups=mesh['runner'=4,'cells'=8] {'runner'}, dimensions={0}, use_global_device_ids=true | all-gather | bytes 1280 | tf_op jit(solution)/shard_map/all_gather | solution.py:99
  108.9 1.9 gather_fusion.5
  110.9 2.9 %gather_fusion.1 = bf16[256,1024]{1,0:T(8,128)(2,1)S(1)} fusion(bf16[512,1024]{1,0:T(8,128)(2,1)} %all-gather.3.cloned.1.call-done, s32[1024]{0:T(1024)S(1)} %pad_clamp_fusion), kind=kCustom, calls=%fused_computation.1 | custom fusion | bytes 1049600 | tf_op jit(solution)/shard_map/jit(_take)/gather | solution.py:81
  114.2 2.0 gather_fusion.2
  116.1 1.1 fusion.11
  118.0 50.6 %all-reduce.2.cloned.1.call-done = f32[128,256]{1,0:T(8,128)} async-done(((f32[128,256]{1,0:T(8,128)}), f32[128,256]{1,0:T(8,128)}) %all-reduce.2.cloned.1.call-update) | async-done | bytes 131088 | tf_op jit(solution)/shard_map/psum | solution.py:89
  168.5 0.9 multiply_convert_fusion
  169.4 13.9 %all_gather.10 = bf16[512,256]{1,0:T(8,128)(2,1)S(1)} all-gather(bf16[128,256]{1,0:T(8,128)(2,1)S(1)} %multiply_convert_fusion), channel_id=1, replica_groups=mesh['runner'=4,'cells'=8] {'runner'}, dimensions={0}, use_global_device_ids=true | all-gather | bytes 327680 | tf_op jit(solution)/shard_map/all_gather | solution.py:98
  183.4 1.2 gather_fusion.3
  185.4 11.7 %psum.39 = f32[1024]{0:T(1024)S(1)} all-reduce(f32[1024]{0:T(1024)S(1)} %bitcast.74), channel_id=1, replica_groups=mesh['runner'=4,'cells'=8] {'runner'}, use_global_device_ids=true, to_apply=%region_11.12 | all-reduce | flops 1024 | bytes 8192 | tf_op jit(solution)/shard_map/psum | solution.py:119
  197.4 0.9 copy.17
  (70 shorter events, 12.3 us)
Async XLA Ops:
  6.5 104.4 %all-gather.3.cloned.1.call-start = ((), (), s32[]{:S(2)}) async-start(), calls=%async_computation | async-start | bytes 1310720 | tf_op jit(solution)/shard_map/all_gather | solution.py:80
  7.3 10.5 %collective-permute-start.2 = (f32[3,4,128]{2,1,0:T(4,128)S(1)}, f32[3,4,128]{2,1,0:T(4,128)S(1)}, u32[]{:S(2)}, u32[]{:S(2)}) collective-permute-start(f32[3,4,128]{2,1,0:T(4,128)S(1)} %get-tuple-element.40), channel_id=1, source_target_pairs={{0,1},{1,2},{2,3},{3,4},{4,5},{5,6},{6,7},{7,0},{8,9},{9,10},{10,1... | collective-permute-start | bytes 18440 | tf_op jit(solution)/shard_map/ppermute | solution.py:15
  7.8 12.2 %copy-start.1 = (f32[128,8,128]{2,1,0:T(8,128)S(1)}, f32[128,8,128]{2,1,0:T(8,128)}, u32[]{:S(2)}) copy-start(f32[128,8,128]{2,1,0:T(8,128)} %param.7) | copy-start | bytes 1572868
  7.8 10.0 %collective-permute-start.3 = (f32[3,4,128]{2,1,0:T(4,128)S(1)}, f32[3,4,128]{2,1,0:T(4,128)S(1)}, u32[]{:S(2)}, u32[]{:S(2)}) collective-permute-start(f32[3,4,128]{2,1,0:T(4,128)S(1)} %get-tuple-element.41), channel_id=1, source_target_pairs={{1,0},{2,1},{3,2},{4,3},{5,4},{6,5},{7,6},{0,7},{9,8},{10,9},{11,1... | collective-permute-start | bytes 18440 | tf_op jit(solution)/shard_map/ppermute | solution.py:18
  10.7 4.0 %copy-start.2 = (f32[2,8,128]{2,1,0:T(8,128)S(1)}, f32[2,8,128]{2,1,0:T(8,128)}, u32[]{:S(2)}) copy-start(f32[2,8,128]{2,1,0:T(8,128)} %param.9) | copy-start | bytes 24580
  12.0 7.9 %collective-permute-start = (f32[128,4,128]{2,1,0:T(4,128)S(1)}, f32[128,4,128]{2,1,0:T(4,128)S(1)}, u32[]{:S(2)}, u32[]{:S(2)}) collective-permute-start(f32[128,4,128]{2,1,0:T(4,128)S(1)} %get-tuple-element.29), channel_id=1, source_target_pairs={{0,1},{1,2},{2,3},{3,4},{4,5},{5,6},{6,7},{7,0},{8,9},{9,10},{10,1... | collective-permute-start | bytes 786440 | tf_op jit(solution)/shard_map/ppermute | solution.py:15
  12.1 7.8 %collective-permute-start.1 = (f32[128,4,128]{2,1,0:T(4,128)S(1)}, f32[128,4,128]{2,1,0:T(4,128)S(1)}, u32[]{:S(2)}, u32[]{:S(2)}) collective-permute-start(f32[128,4,128]{2,1,0:T(4,128)S(1)} %get-tuple-element.30), channel_id=1, source_target_pairs={{1,0},{2,1},{3,2},{4,3},{5,4},{6,5},{7,6},{0,7},{9,8},{10,9},{11,1... | collective-permute-start | bytes 786440 | tf_op jit(solution)/shard_map/ppermute | solution.py:18
  14.8 0.7 copy-start.4
  15.4 0.7 copy-start.7
  17.1 0.8 copy-start.3
  41.2 0.9 copy-start
  41.2 127.3 %all-reduce.2.cloned.1.call-start = ((), (), s32[]{:S(2)}) async-start(), calls=%async_computation.1 | async-start | bytes 262144 | tf_op jit(solution)/shard_map/psum | solution.py:89
  44.6 1.4 copy-start.6
  44.6 1.4 copy-start.5
Sparse Core Ops, SparseCore 0:
  41.3 26.5 all-gather.2
  117.4 51.1 all-reduce.1
where the time goes:
time: 206 us; the launch traced here: 205 us
  blocking collectives  100 us (49%)
  waiting for transfers between devices  52.7 us (26%)
  local copies, waits for them, and re-layouts  18.9 us (9%)
  between operations  14.3 us (7%)
  other arithmetic  10.4 us (5%)
  starting transfers between devices  6.15 us (3%)
  matrix products  2.57 us (1%)
    psum x1, waiting for transfers between devices, body(): gram_rows, bias_rows = lax.psum((gram_part, bias_part), 'cells')  50.6 us
    psum x1, blocking collectives, body(): lax.psum(jnp.sum(weighted.astype(jnp.float32) * own_obs.astype(jnp.float3...  38.3 us
    all_gather x1, blocking collectives, body(): lax.all_gather(scaled_own, 'runner', axis=0, tiled=True)  13.9 us
    psum x1, blocking collectives, body(): ensemble_mean = lax.psum(live_sum, 'runner') / members  13.4 us
    psum x1, blocking collectives, body(): gram_rows, bias_rows = lax.psum((gram_part, bias_part), 'cells')  12.9 us
    psum x1, blocking collectives, body(): lax.psum(jnp.dot(shift_weights, member_deviation.astype(jnp.float32), pre...  11.7 us
    all_gather x1, blocking collectives, body(): lax.all_gather(bias_own, 'runner', axis=0, tiled=True)  9.94 us
    ppermute x2, starting transfers between devices, with_halo(): lax.ppermute(lax.slice_in_dim(block, 0, width, axis=dim), axis, backward)  5.56 us
  transfers between devices with their start and end apart: 6, of which 2 were waited for; matrix products, arithmetic and copies ran while one was open for 5% of the time, Pallas kernels for 0%

commit v1 on v0

--- a/solution.py
+++ b/solution.py
@@ -4,6 +4,27 @@
 from jax.sharding import PartitionSpec as P
 
 STEPS = 4
+
+
+def step_on_the_lane(field_in, in_dim):
+    top = list(field_in.shape[1:])
+    top[in_dim] *= field_in.shape[0]
+    q_next = jnp.moveaxis(field_in, 0, in_dim).reshape(top)
+    return q_next
+
+
+def launch_the_stages_all(field, mesh_ax, along_dim):
+    full_n = lax.psum(1, mesh_ax)
+    log = []
+    for m in tuple(range(full_n)):
+        log.append((m, (m + 1) % full_n))
+    views = [field]
+    while len(views) < full_n:
+        views.append(lax.ppermute(views[-1], mesh_ax, log))
+    local_next = lax.axis_index(mesh_ax)
+    views = jnp.stack(views)[(local_next - jnp.arange(full_n)) % full_n]
+    mid_arr = step_on_the_lane(views, along_dim)
+    return mid_arr
 
 
 def with_halo(block, sides, width):
@@ -95,7 +116,7 @@
     scaled_own = (gram_rows * scaling).astype(jnp.bfloat16)
     bias_own = (bias_rows * scaling).astype(jnp.bfloat16)
     scaled_all, bias_all = (
-        lax.all_gather(scaled_own, "runner", axis=0, tiled=True),
+        launch_the_stages_all(scaled_own, mesh_ax="runner", along_dim=0),
         lax.all_gather(bias_own, "runner", axis=0, tiled=True),
     )
     scaled_full = jnp.take(scaled_all, slot_of, axis=0)

time: 206 us -> 208 us (level)
  blocking collectives: 100 us -> 82.9 us
  waiting for transfers between devices: 52.7 us -> 69.4 us
    ppermute x0 -> x3, waiting for transfers between devices: none -> 16 us  [launch_the_stages_all(): views.append(lax.ppermute(views[-1], mesh_ax, log))]
    all_gather x1 -> x0, blocking collectives: 13.9 us -> none  [body(): lax.all_gather(scaled_own, 'runner', axis=0, tiled=True)]
    psum x1, blocking collectives: 11.7 us -> 8.35 us  [body(): lax.psum(jnp.dot(shift_weights, member_deviation.astype(jnp.float32), pre...]
  transfers between devices with their start and end apart: 6 -> 9, of which waited for: 2 -> 5; matrix products, arithmetic and copies ran while one was open for 5% -> 5% of each run, Pallas kernels for 0% -> 0%
where the time goes in v1:
time: 208 us; the launch traced here: 207 us
  blocking collectives  82.9 us (40%)
  waiting for transfers between devices  69.4 us (33%)
  local copies, waits for them, and re-layouts  19.5 us (9%)
  between operations  14.4 us (7%)
  other arithmetic  10.4 us (5%)
  starting transfers between devices  7.69 us (4%)
  matrix products  2.57 us (1%)
    psum x1, waiting for transfers between devices, body(): gram_rows, bias_rows = lax.psum((gram_part, bias_part), 'cells')  51.2 us
    psum x1, blocking collectives, body(): lax.psum(jnp.sum(weighted.astype(jnp.float32) * own_obs.astype(jnp.float3...  38.4 us
    ppermute x3, waiting for transfers between devices, launch_the_stages_all(): views.append(lax.ppermute(views[-1], mesh_ax, log))  16 us
    psum x1, blocking collectives, body(): ensemble_mean = lax.psum(live_sum, 'runner') / members  13.4 us
    psum x1, blocking collectives, body(): gram_rows, bias_rows = lax.psum((gram_part, bias_part), 'cells')  12.9 us
    all_gather x1, blocking collectives, body(): lax.all_gather(bias_own, 'runner', axis=0, tiled=True)  9.9 us
    psum x1, blocking collectives, body(): lax.psum(jnp.dot(shift_weights, member_deviation.astype(jnp.float32), pre...  8.35 us
    ppermute x2, starting transfers between devices, with_halo(): lax.ppermute(lax.slice_in_dim(block, 0, width, axis=dim), axis, backward)  5.56 us
  transfers between devices with their start and end apart: 9, of which 5 were waited for; matrix products, arithmetic and copies ran while one was open for 5% of the time, Pallas kernels for 0%

profile of v1, /device:TPU:0, one launch (start us, length us, event | category | flops | bytes accessed | tf_op | source)
XLA Modules:
  0.0 207.0 jit_solution(7652261775394831259)
XLA Ops:
  7.8 2.9 %collective-permute-start.3 = (f32[3,4,128]{2,1,0:T(4,128)S(1)}, f32[3,4,128]{2,1,0:T(4,128)S(1)}, u32[]{:S(2)}, u32[]{:S(2)}) collective-permute-start(f32[3,4,128]{2,1,0:T(4,128)S(1)} %get-tuple-element.41), channel_id=1, source_target_pairs={{1,0},{2,1},{3,2},{4,3},{5,4},{6,5},{7,6},{0,7},{9,8},{10,9},{11,1... | collective-permute-start | bytes 18440 | tf_op jit(solution)/shard_map/ppermute | solution.py:39
  10.7 1.3 fusion.43
  12.1 2.6 %collective-permute-start.1 = (f32[128,4,128]{2,1,0:T(4,128)S(1)}, f32[128,4,128]{2,1,0:T(4,128)S(1)}, u32[]{:S(2)}, u32[]{:S(2)}) collective-permute-start(f32[128,4,128]{2,1,0:T(4,128)S(1)} %get-tuple-element.30), channel_id=1, source_target_pairs={{1,0},{2,1},{3,2},{4,3},{5,4},{6,5},{7,6},{0,7},{9,8},{10,9},{11,1... | collective-permute-start | bytes 786440 | tf_op jit(solution)/shard_map/ppermute | solution.py:39
  17.9 2.1 %collective-permute-done = f32[128,4,128]{2,1,0:T(4,128)S(1)} collective-permute-done((f32[128,4,128]{2,1,0:T(4,128)S(1)}, f32[128,4,128]{2,1,0:T(4,128)S(1)}, u32[]{:S(2)}, u32[]{:S(2)}) %collective-permute-start) | collective-permute-done | bytes 262176 | tf_op jit(solution)/shard_map/ppermute | solution.py:36
  20.9 1.2 fusion.3
  22.8 1.2 fusion.4
  24.7 1.2 fusion.5
  27.0 13.4 %psum.35 = f32[1024]{0:T(1024)S(1)} all-reduce(f32[1024]{0:T(1024)S(1)} %bitcast.87), channel_id=1, replica_groups=mesh['runner'=4,'cells'=8] {'runner'}, use_global_device_ids=true, to_apply=%region_2.3 | all-reduce | flops 1024 | bytes 8192 | tf_op jit(solution)/shard_map/psum | solution.py:90
  42.3 2.3 %gather_fusion.5 = f32[512]{0:T(512)S(1)} fusion(f32[1024]{0:T(1024)S(1)} %broadcast_multiply_fusion, s32[1024]{0:T(1024)S(1)} %pad_clamp_fusion.2), kind=kCustom, calls=%fused_computation.5 | custom fusion | bytes 6144 | tf_op jit(solution)/shard_map/jit(_take)/gather | solution.py:108
  44.6 1.3 gather_fusion
  46.9 38.4 %psum.37 = f32[]{:T(128)} all-reduce(f32[]{:T(128)} %fusion.10), channel_id=1, replica_groups=mesh['runner'=4,'cells'=8] {'runner','cells'}, use_global_device_ids=true, to_apply=%region_9.10 | all-reduce | flops 1 | bytes 8 | tf_op jit(solution)/shard_map/psum | solution.py:112
  86.3 12.9 %psum.38 = f32[128]{0:T(128)S(1)} all-reduce(f32[128]{0:T(128)S(1)} %convolution_bitcast_fusion), channel_id=1, replica_groups=mesh['runner'=4,'cells'=8] {'cells'}, use_global_device_ids=true, to_apply=%region_10.11 | all-reduce | flops 128 | bytes 1024 | tf_op jit(solution)/shard_map/psum | solution.py:110
  99.3 9.9 %all-gather = bf16[4,1,128]{2,1,0:T(2,128)(2,1)S(1)} all-gather(bf16[1,1,128]{2,1,0:T(2,128)(2,1)S(1)} %convert_bitcast_fusion), channel_id=1, replica_groups=mesh['runner'=4,'cells'=8] {'runner'}, dimensions={0}, use_global_device_ids=true | all-gather | bytes 1280 | tf_op jit(solution)/shard_map/all_gather | solution.py:120
  109.2 1.9 gather_fusion.6
  111.2 2.9 %gather_fusion.1 = bf16[256,1024]{1,0:T(8,128)(2,1)S(1)} fusion(bf16[512,1024]{1,0:T(8,128)(2,1)} %all-gather.3.cloned.1.call-done, s32[1024]{0:T(1024)S(1)} %pad_clamp_fusion.1), kind=kCustom, calls=%fused_computation.1 | custom fusion | bytes 1049600 | tf_op jit(solution)/shard_map/jit(_take)/gather | solution.py:102
  114.4 2.0 gather_fusion.2
  116.4 1.1 fusion.11
  117.5 51.2 %all-reduce.2.cloned.1.call-done = f32[128,256]{1,0:T(8,128)} async-done(((f32[128,256]{1,0:T(8,128)}), f32[128,256]{1,0:T(8,128)}) %all-reduce.2.cloned.1.call-update) | async-done | bytes 131088 | tf_op jit(solution)/shard_map/psum | solution.py:110
  169.8 1.5 collective-permute-start.4
  171.3 4.6 %collective-permute-done.4 = bf16[128,256]{1,0:T(8,128)(2,1)S(1)} collective-permute-done((bf16[128,256]{1,0:T(8,128)(2,1)S(1)}, bf16[128,256]{1,0:T(8,128)(2,1)S(1)}, u32[]{:S(2)}, u32[]{:S(2)}) %collective-permute-start.4) | collective-permute-done | bytes 65568 | tf_op jit(solution)/shard_map/ppermute | solution.py:23
  176.5 5.4 %collective-permute-done.5 = bf16[128,256]{1,0:T(8,128)(2,1)S(1)} collective-permute-done((bf16[128,256]{1,0:T(8,128)(2,1)S(1)}, bf16[128,256]{1,0:T(8,128)(2,1)S(1)}, u32[]{:S(2)}, u32[]{:S(2)}) %collective-permute-start.5) | collective-permute-done | bytes 65568 | tf_op jit(solution)/shard_map/ppermute | solution.py:23
  182.0 6.0 %collective-permute-done.6 = bf16[128,256]{1,0:T(8,128)(2,1)S(1)} collective-permute-done((bf16[128,256]{1,0:T(8,128)(2,1)S(1)}, bf16[128,256]{1,0:T(8,128)(2,1)S(1)}, u32[]{:S(2)}, u32[]{:S(2)}) %collective-permute-start.6) | collective-permute-done | bytes 65568 | tf_op jit(solution)/shard_map/ppermute | solution.py:23
  188.6 1.2 gather_fusion.4
  190.7 8.3 %psum.39 = f32[1024]{0:T(1024)S(1)} all-reduce(f32[1024]{0:T(1024)S(1)} %bitcast.86), channel_id=1, replica_groups=mesh['runner'=4,'cells'=8] {'runner'}, use_global_device_ids=true, to_apply=%region_11.12 | all-reduce | flops 1024 | bytes 8192 | tf_op jit(solution)/shard_map/psum | solution.py:140
  (82 shorter events, 15.6 us)
Async XLA Ops:
  6.5 104.6 %all-gather.3.cloned.1.call-start = ((), (), s32[]{:S(2)}) async-start(), calls=%async_computation | async-start | bytes 1310720 | tf_op jit(solution)/shard_map/all_gather | solution.py:101
  7.3 10.4 %collective-permute-start.2 = (f32[3,4,128]{2,1,0:T(4,128)S(1)}, f32[3,4,128]{2,1,0:T(4,128)S(1)}, u32[]{:S(2)}, u32[]{:S(2)}) collective-permute-start(f32[3,4,128]{2,1,0:T(4,128)S(1)} %get-tuple-element.40), channel_id=1, source_target_pairs={{0,1},{1,2},{2,3},{3,4},{4,5},{5,6},{6,7},{7,0},{8,9},{9,10},{10,1... | collective-permute-start | bytes 18440 | tf_op jit(solution)/shard_map/ppermute | solution.py:36
  7.8 12.2 %copy-start.1 = (f32[128,8,128]{2,1,0:T(8,128)S(1)}, f32[128,8,128]{2,1,0:T(8,128)}, u32[]{:S(2)}) copy-start(f32[128,8,128]{2,1,0:T(8,128)} %param.7) | copy-start | bytes 1572868
  7.8 10.0 %collective-permute-start.3 = (f32[3,4,128]{2,1,0:T(4,128)S(1)}, f32[3,4,128]{2,1,0:T(4,128)S(1)}, u32[]{:S(2)}, u32[]{:S(2)}) collective-permute-start(f32[3,4,128]{2,1,0:T(4,128)S(1)} %get-tuple-element.41), channel_id=1, source_target_pairs={{1,0},{2,1},{3,2},{4,3},{5,4},{6,5},{7,6},{0,7},{9,8},{10,9},{11,1... | collective-permute-start | bytes 18440 | tf_op jit(solution)/shard_map/ppermute | solution.py:39
  10.7 4.0 %copy-start.3 = (f32[2,8,128]{2,1,0:T(8,128)S(1)}, f32[2,8,128]{2,1,0:T(8,128)}, u32[]{:S(2)}) copy-start(f32[2,8,128]{2,1,0:T(8,128)} %param.9) | copy-start | bytes 24580
  12.0 7.9 %collective-permute-start = (f32[128,4,128]{2,1,0:T(4,128)S(1)}, f32[128,4,128]{2,1,0:T(4,128)S(1)}, u32[]{:S(2)}, u32[]{:S(2)}) collective-permute-start(f32[128,4,128]{2,1,0:T(4,128)S(1)} %get-tuple-element.29), channel_id=1, source_target_pairs={{0,1},{1,2},{2,3},{3,4},{4,5},{5,6},{6,7},{7,0},{8,9},{9,10},{10,1... | collective-permute-start | bytes 786440 | tf_op jit(solution)/shard_map/ppermute | solution.py:36
  12.1 7.8 %collective-permute-start.1 = (f32[128,4,128]{2,1,0:T(4,128)S(1)}, f32[128,4,128]{2,1,0:T(4,128)S(1)}, u32[]{:S(2)}, u32[]{:S(2)}) collective-permute-start(f32[128,4,128]{2,1,0:T(4,128)S(1)} %get-tuple-element.30), channel_id=1, source_target_pairs={{1,0},{2,1},{3,2},{4,3},{5,4},{6,5},{7,6},{0,7},{9,8},{10,9},{11,1... | collective-permute-start | bytes 786440 | tf_op jit(solution)/shard_map/ppermute | solution.py:39
  14.8 0.7 copy-start.5
  15.4 0.7 copy-start.8
  17.0 0.8 copy-start.4
  41.2 0.9 copy-start
  41.2 127.6 %all-reduce.2.cloned.1.call-start = ((), (), s32[]{:S(2)}) async-start(), calls=%async_computation.1 | async-start | bytes 262144 | tf_op jit(solution)/shard_map/psum | solution.py:110
  44.6 1.4 copy-start.7
  44.6 1.4 copy-start.6
  168.8 13.2 %copy-start.2 = (f32[128,256]{1,0:T(8,128)S(1)}, f32[128,256]{1,0:T(8,128)}, u32[]{:S(2)}) copy-start(f32[128,256]{1,0:T(8,128)} %all-reduce.2.cloned.1.call-done) | copy-start | bytes 393220
  169.8 6.1 %collective-permute-start.4 = (bf16[128,256]{1,0:T(8,128)(2,1)S(1)}, bf16[128,256]{1,0:T(8,128)(2,1)S(1)}, u32[]{:S(2)}, u32[]{:S(2)}) collective-permute-start(bf16[128,256]{1,0:T(8,128)(2,1)S(1)} %multiply_convert_fusion), channel_id=1, source_target_pairs={{0,8},{8,16},{16,24},{24,0},{1,9},{9,17},{17,25},{25,1},{2,10},{10... | collective-permute-start | bytes 196616 | tf_op jit(solution)/shard_map/ppermute | solution.py:23
  175.9 6.1 %collective-permute-start.5 = (bf16[128,256]{1,0:T(8,128)(2,1)S(1)}, bf16[128,256]{1,0:T(8,128)(2,1)S(1)}, u32[]{:S(2)}, u32[]{:S(2)}) collective-permute-start(bf16[128,256]{1,0:T(8,128)(2,1)S(1)} %collective-permute-done.4), channel_id=1, source_target_pairs={{0,8},{8,16},{16,24},{24,0},{1,9},{9,17},{17,25},{25,1},{2,10},{10... | collective-permute-start | bytes 196616 | tf_op jit(solution)/shard_map/ppermute | solution.py:23
  182.0 6.1 %collective-permute-start.6 = (bf16[128,256]{1,0:T(8,128)(2,1)S(1)}, bf16[128,256]{1,0:T(8,128)(2,1)S(1)}, u32[]{:S(2)}, u32[]{:S(2)}) collective-permute-start(bf16[128,256]{1,0:T(8,128)(2,1)S(1)} %collective-permute-done.5), channel_id=1, source_target_pairs={{0,8},{8,16},{16,24},{24,0},{1,9},{9,17},{17,25},{25,1},{2,10},{10... | collective-permute-start | bytes 196616 | tf_op jit(solution)/shard_map/ppermute | solution.py:23
Sparse Core Ops, SparseCore 0:
  41.3 26.5 all-gather.2
  117.6 51.0 all-reduce.1
